TPU v7x, 32 devices: a whole 2x2x4 slice. The times are simulated.
32 devices in a mesh: band: 8 (over z, y), mode: 4 (over x, core).
Axes of the slice: x: 2, y: 2, z: 4, core: 2. Of those that a mesh axis runs over, the one named last changes fastest.
Arguments:
- velocity: bfloat16 [1, 8192, 1024], P(None, ('band', 'mode')), may hold values from -6 to 6
- radiation_modes: bfloat16 [8192, 1024], P('band', 'mode'), may hold values from -0.125 to 0.125
- resistance: float32 [8, 1024, 1024], P('band', None, 'mode'), as said below
- mode_ranks: int32 [8], P('band'), may hold values from 128 to 1024, as said below
- freq_table: int32 [512], replicated, may hold values from 0 to 511, each once
Outputs:
- adjoint_force: bfloat16 [1, 8192, 1024], P(None, ('band', 'mode'))
Inputs may be any that keep to these rules, and one draw needn't show every extreme that they name: `resistance`: each band's matrix is symmetric. `mode_ranks`: the ranks never fall with the band index; the first band keeps 1024 // 8 modes and the last 1024.
All inputs are finite; a program needn't handle non-finite values.
Results may differ from a plain program's by a relative error of at most 0.015.
Values may be sent and summed in bfloat16 or wider, within the bound.
A program may use at most 64 MiB of HBM per device.

v0:
```python
import math
import jax
import jax.numpy as jnp
from jax import lax
from jax.sharding import PartitionSpec as P


def make_table(freq_table, step_count):
    times = jnp.arange(step_count, dtype=jnp.int32)
    phases = times[:, None] * freq_table[None, :] % step_count
    angles = phases.astype(jnp.float32) * (2.0 * math.pi / step_count)
    norming = 1.0 / math.sqrt(step_count)
    table = jnp.stack([jnp.cos(angles), -jnp.sin(angles)], axis=1) * norming
    return table.astype(jnp.bfloat16)


def add_sources(received):
    return jnp.sum(received, axis=0)


def per_device(velocity, radiation_modes, resistance, mode_ranks, freq_table):
    step_count = velocity.shape[2]
    mode_cols = radiation_modes.shape[1]
    dft_table = make_table(freq_table, step_count)
    spectra = jnp.einsum(
        "wpt,tcf->wpcf", velocity, dft_table, preferred_element_type=jnp.float32
    ).astype(jnp.bfloat16)
    partial_value = jnp.einsum(
        "wpcf,pr->wrcf",
        lax.all_gather(spectra, "mode", axis=1, tiled=True),
        radiation_modes,
        preferred_element_type=jnp.float32,
    )
    coefficients = add_sources(
        lax.all_to_all(
            partial_value[None].astype(jnp.bfloat16),
            "band",
            split_axis=4,
            concat_axis=0,
            tiled=True,
        ).astype(jnp.float32)
    )
    offset = lax.axis_index("mode") * mode_cols
    rank_here = mode_ranks[0]
    kept_mask = (offset + jnp.arange(mode_cols, dtype=jnp.int32) < rank_here).astype(jnp.float32)
    kept_mask = kept_mask[None, :, None, None]
    coefficients = coefficients * kept_mask
    matrix = resistance[0]
    partial_terms = jnp.einsum(
        "ij,wjcf->wicf", matrix, coefficients, precision=lax.Precision.HIGHEST
    )
    forcing = lax.psum_scatter(
        partial_terms.astype(jnp.bfloat16), "mode", scatter_dimension=1, tiled=True
    ).astype(jnp.float32)
    forcing = (2.0 * forcing * kept_mask).astype(jnp.bfloat16)
    collected = lax.all_gather(forcing, "mode", axis=1, tiled=True)
    collected = lax.all_gather(collected, "band", axis=3, tiled=True)
    own_basis = lax.all_to_all(radiation_modes, "mode", split_axis=0, concat_axis=1, tiled=True)
    surface_force = jnp.einsum(
        "pr,wrcf->wpcf", own_basis, collected, preferred_element_type=jnp.float32
    ).astype(jnp.bfloat16)
    history = jnp.einsum(
        "wpcf,tcf->wpt", surface_force, dft_table, preferred_element_type=jnp.float32
    )
    return history.astype(jnp.bfloat16)


def solution(mesh):
    placed = (
        P(None, ("band", "mode"), None),
        P("band", "mode"),
        P("band", None, "mode"),
        P("band"),
        P(),
    )
    return jax.shard_map(
        per_device,
        mesh=mesh,
        in_specs=placed,
        out_specs=P(None, ("band", "mode"), None),
        check_vma=False,
    )
```

profile of v0, /device:TPU:0, one launch (start us, length us, event | category | flops | bytes accessed | tf_op | source)
XLA Modules:
  0.0 158.5 jit_solution(3879735066893673971)
XLA Ops:
  6.5 0.0 copy-start
  6.5 0.0 copy-start.4
  6.5 0.0 all-gather.6.cloned.1.call-start
  6.5 9.1 %fusion.21 = (f32[1024,1,512]{0,2,1:T(8,128)S(1)}, f32[1024,1,512]{0,2,1:T(8,128)S(1)}) fusion(s32[512]{0:T(512)} %param.9), kind=kLoop, calls=%fused_computation.27 | loop fusion | flops 7864320 | bytes 4196352 | tf_op jit(solution)/shard_map/cos | solution.py:13
  15.7 0.0 copy-start.1
  15.7 0.0 copy-start.2
  15.7 1.3 copy-done.1
  17.0 0.6 copy-done.2
  17.6 0.0 copy-done.4
  17.7 1.6 fusion.13
  19.2 0.0 all-gather.6.cloned.1.call-update
  19.2 25.7 %all-gather.6.cloned.1.call-done = bf16[1024,2,512]{0,2,1:T(8,128)(2,1)} async-done(((bf16[256,2,512]{0,2,1:T(8,128)(2,1)}), bf16[1024,2,512]{0,2,1:T(8,128)(2,1)}) %all-gather.6.cloned.1.call-update) | async-done | bytes 2097168 | tf_op jit(solution)/shard_map/all_gather | solution.py:30
  44.9 0.0 copy-done.3
  44.9 2.3 %fusion.14 = bf16[1,1,256,2,512]{2,4,3,1,0:T(8,128)(2,1)S(1)} fusion(bf16[1024,2,512]{0,2,1:T(8,128)(2,1)} %all-gather.6.cloned.1.call-done, bf16[1024,256]{1,0:T(8,128)(2,1)S(1)} %copy-done.3), kind=kOutput, calls=%fused_computation.20 | convolution fusion | flops 537133056 | bytes 3145728 | tf_op jit(solution)/shard_map/wpcf,pr->wrcf/dot_general | solution.py:28
  47.2 1.3 copy.16
  48.6 5.5 %all-to-all-start = ((bf16[1,1,256,2,512]{2,3,1,0,4:T(2,128)(2,1)}), bf16[1,1,256,2,512]{2,3,1,0,4:T(2,128)(2,1)S(1)}, u32[]{:S(2)}, u32[]{:S(2)}) async-start(bf16[1,1,256,2,512]{2,3,1,0,4:T(2,128)(2,1)} %copy.16), calls=%async_computation | async-start | bytes 1048576 | tf_op jit(solution)/shard_map/all_to_all | solution.py:35
  54.1 0.2 reduce-scatter.2.cloned.1.call-start
  55.0 14.0 %all-to-all-done = bf16[1,1,256,2,512]{2,3,1,0,4:T(2,128)(2,1)S(1)} async-done(((bf16[1,1,256,2,512]{2,3,1,0,4:T(2,128)(2,1)}), bf16[1,1,256,2,512]{2,3,1,0,4:T(2,128)(2,1)S(1)}, u32[]{:S(2)}, u32[]{:S(2)}) %all-to-all-start) | async-done | bytes 524320 | tf_op jit(solution)/shard_map/all_to_all | solution.py:35
  69.0 0.5 convert_reduce_fusion
  69.4 0.0 copy-done
  69.5 1.9 %fusion.19 = bf16[1,1024,2,64]{1,3,2,0:T(8,128)(2,1)} fusion(f32[1,1024,256]{2,1,0:T(8,128)S(1)} %copy-done, f32[256,2,64]{0,1,2:T(2,128)S(1)} %convert_reduce_fusion, f32[256]{0:T(256)S(1)} %fusion.30), kind=kOutput, calls=%fused_computation.24 | convolution fusion | flops 402817024 | bytes 1442816 | tf_op jit(solution)/shard_map/ij,wjcf->wicf/dot_general | solution.py:49
  71.4 0.0 reduce-scatter.2.cloned.1.call-update
  71.4 0.0 all-gather.4.cloned.1.call-start
  71.5 18.3 %reduce-scatter.2.cloned.1.call-done = bf16[1,256,2,64]{1,3,2,0:T(8,128)(2,1)} async-done(((bf16[1,1024,2,64]{1,3,2,0:T(8,128)(2,1)}), bf16[1,256,2,64]{1,3,2,0:T(8,128)(2,1)}) %reduce-scatter.2.cloned.1.call-update) | async-done | bytes 65552 | tf_op jit(solution)/shard_map/reduce_scatter | solution.py:52
  89.7 0.9 multiply_convert_fusion
  90.6 6.2 %all_gather.10 = bf16[1,1024,2,64]{1,3,2,0:T(8,128)(2,1)} all-gather(bf16[1,256,2,64]{1,3,2,0:T(8,128)(2,1)S(1)} %multiply_convert_fusion), channel_id=1, replica_groups=mesh['band'=8,'mode'=4] {'mode'}, dimensions={1}, use_global_device_ids=true | all-gather | bytes 327680 | tf_op jit(solution)/shard_map/all_gather | solution.py:56
  96.8 0.0 all-gather.4.cloned.1.call-update
  96.8 11.2 %all_to_all.28 = bf16[4,256,256]{2,1,0:T(8,128)(2,1)S(1)} all-to-all(bf16[4,256,256]{2,1,0:T(8,128)(2,1)S(1)} %bitcast.57), channel_id=1, replica_groups=mesh['band'=8,'mode'=4] {'mode'}, dimensions={0} | all-to-all | bytes 1048576 | tf_op jit(solution)/shard_map/all_to_all | solution.py:58
  108.1 0.4 copy.18
  108.5 0.4 reshape.162
  108.8 37.2 %all-gather.4.cloned.1.call-done = bf16[1,1024,2,512]{1,3,2,0:T(8,128)(2,1)} async-done(((bf16[1,1024,2,64]{1,3,2,0:T(8,128)(2,1)}), bf16[1,1024,2,512]{1,3,2,0:T(8,128)(2,1)}) %all-gather.4.cloned.1.call-update) | async-done | bytes 2097168 | tf_op jit(solution)/shard_map/all_gather | solution.py:57
  146.1 5.9 %fusion.18 = bf16[1,256,1024]{2,1,0:T(8,128)(2,1)} fusion(bf16[256,1024,1]{1,0,2:T(8,128)(2,1)S(1)} %reshape.162, bf16[1,1024,2,512]{1,3,2,0:T(8,128)(2,1)} %all-gather.4.cloned.1.call-done, f32[1024,1,512]{0,2,1:T(8,128)} %copy-done.2, f32[1024,1,512]{0,2,1:T(8,128)} %copy-done.1), kind=kOutput, calls=%fused_computation.22 | convolution fusion | flops 1077411840 | bytes 7340032 | tf_op jit(solution)/shard_map/wpcf,tcf->wpt/dot_general | solution.py:62
  (3 shorter events, 0.0 us)
Async XLA Ops:
  6.5 62.9 %copy-start = (f32[1,1024,256]{2,1,0:T(8,128)S(1)}, f32[1,1024,256]{2,1,0:T(8,128)}, u32[]{:S(2)}) copy-start(f32[1,1024,256]{2,1,0:T(8,128)} %param.7) | copy-start | bytes 3145732
  6.5 11.1 %copy-start.4 = (bf16[1,256,1024]{2,1,0:T(8,128)(2,1)S(1)}, bf16[1,256,1024]{2,1,0:T(8,128)(2,1)}, u32[]{:S(2)}) copy-start(bf16[1,256,1024]{2,1,0:T(8,128)(2,1)} %param.5) | copy-start | bytes 1572868
  6.5 38.4 %all-gather.6.cloned.1.call-start = ((), (), s32[]{:S(2)}) async-start(), calls=%async_computation.5 | async-start | bytes 2621440 | tf_op jit(solution)/shard_map/all_gather | solution.py:30
  15.7 1.3 copy-start.1
  15.7 1.9 %copy-start.2 = (f32[1024,1,512]{0,2,1:T(8,128)}, f32[1024,1,512]{0,2,1:T(8,128)S(1)}, u32[]{:S(2)}) copy-start(f32[1024,1,512]{0,2,1:T(8,128)S(1)} %get-tuple-element.6) | copy-start | bytes 6291460
  17.7 27.3 %copy-start.3 = (bf16[1024,256]{1,0:T(8,128)(2,1)S(1)}, bf16[1024,256]{1,0:T(8,128)(2,1)}, u32[]{:S(2)}) copy-start(bf16[1024,256]{1,0:T(8,128)(2,1)} %param.6) | copy-start | bytes 1572868
  48.6 20.4 %all-to-all-start = ((bf16[1,1,256,2,512]{2,3,1,0,4:T(2,128)(2,1)}), bf16[1,1,256,2,512]{2,3,1,0,4:T(2,128)(2,1)S(1)}, u32[]{:S(2)}, u32[]{:S(2)}) async-start(bf16[1,1,256,2,512]{2,3,1,0,4:T(2,128)(2,1)} %copy.16), calls=%async_computation | async-start | bytes 1048576 | tf_op jit(solution)/shard_map/all_to_all | solution.py:35
  54.1 35.7 %reduce-scatter.2.cloned.1.call-start = ((), (), s32[]{:S(2)}) async-start(), calls=%async_computation.3 | async-start | bytes 327680 | tf_op jit(solution)/shard_map/reduce_scatter | solution.py:52
  71.4 74.7 %all-gather.4.cloned.1.call-start = ((), (), s32[]{:S(2)}) async-start(), calls=%async_computation.4 | async-start | bytes 2359296 | tf_op jit(solution)/shard_map/all_gather | solution.py:57
Sparse Core Ops, SparseCore 0:
  19.4 25.5 all-gather.5
  71.5 18.1 reduce-scatter.1
  97.0 49.0 all-gather.3
where the time goes:
time: 159 us
  waiting for transfers between devices  95.3 us (60%)
  blocking collectives  17.4 us (11%)
  between operations  13.8 us (9%)
  matrix products  11.7 us (7%)
  other arithmetic  10.5 us (7%)
  starting transfers between devices  5.78 us (4%)
  local copies, waits for them, and re-layouts  4.06 us (3%)
    all_gather x1, waiting for transfers between devices, per_device(): collected = lax.all_gather(collected, 'band', axis=3, tiled=True)  37.2 us
    all_gather x1, waiting for transfers between devices, per_device(): lax.all_gather(spectra, 'mode', axis=1, tiled=True)  25.7 us
    reduce_scatter x1, waiting for transfers between devices, per_device(): lax.psum_scatter(partial_terms.astype(jnp.bfloat16), 'mode', scatter_dime...  18.3 us
    all_to_all x1, waiting for transfers between devices, per_device(): lax.all_to_all(partial_value[None].astype(jnp.bfloat16), 'band', split_ax...  14 us
    all_to_all x1, blocking collectives, per_device(): lax.all_to_all(radiation_modes, 'mode', split_axis=0, concat_axis=1, tile...  11.2 us
    cos x1, other arithmetic, make_table(): table = jnp.stack([jnp.cos(angles), -jnp.sin(angles)], axis=1) * norming  9.14 us
    all_gather x1, blocking collectives, per_device(): collected = lax.all_gather(forcing, 'mode', axis=1, tiled=True)  6.23 us
    dot_general x1, matrix products, per_device(): jnp.einsum('wpcf,tcf->wpt', surface_force, dft_table, preferred_element_t...  5.95 us
  transfers between devices with their start and end apart: 4, of which 4 were waited for; matrix products, arithmetic and copies ran while one was open for 0% of the time, Pallas kernels for 0%

commit v1 on v0

--- a/solution.py
+++ b/solution.py
@@ -25,12 +25,38 @@
     spectra = jnp.einsum(
         "wpt,tcf->wpcf", velocity, dft_table, preferred_element_type=jnp.float32
     ).astype(jnp.bfloat16)
-    partial_value = jnp.einsum(
+    devices, here, width = (lax.axis_size("mode"), lax.axis_index("mode"), spectra.shape[1])
+    upward = [(i, (i + 1) % devices) for i in range(devices)]
+    left = [(i, (i - 1) % devices) for i in range(devices)]
+    middle = devices // 2
+    from_left = from_right = spectra
+    total = jnp.einsum(
         "wpcf,pr->wrcf",
-        lax.all_gather(spectra, "mode", axis=1, tiled=True),
-        radiation_modes,
+        spectra,
+        lax.dynamic_slice_in_dim(radiation_modes, here * width, spectra.shape[1], axis=0),
         preferred_element_type=jnp.float32,
     )
+    for hop in range(1, middle + 1):
+        from_left = lax.ppermute(from_left, "mode", upward)
+        if hop < devices - middle:
+            from_right = lax.ppermute(from_right, "mode", left)
+            total = total + jnp.einsum(
+                "wpcf,pr->wrcf",
+                from_right,
+                lax.dynamic_slice_in_dim(
+                    radiation_modes, (here + hop) % devices * width, from_right.shape[1], axis=0
+                ),
+                preferred_element_type=jnp.float32,
+            )
+        total = total + jnp.einsum(
+            "wpcf,pr->wrcf",
+            from_left,
+            lax.dynamic_slice_in_dim(
+                radiation_modes, (here - hop) % devices * width, from_left.shape[1], axis=0
+            ),
+            preferred_element_type=jnp.float32,
+        )
+    partial_value = total
     coefficients = add_sources(
         lax.all_to_all(
             partial_value[None].astype(jnp.bfloat16),

time: 159 us -> 152 us (0.956)
  waiting for transfers between devices: 95.3 us -> 84.3 us
  starting transfers between devices: 5.78 us -> 12.6 us
  matrix products: 11.7 us -> 10 us
    all_gather x1 -> x0, waiting for transfers between devices: 25.7 us -> none  [per_device(): lax.all_gather(spectra, 'mode', axis=1, tiled=True)]
    ppermute x0 -> x3, waiting for transfers between devices: none -> 14.9 us  [the longest x2 14.9 us: per_device(): from_left = lax.ppermute(from_left, 'mode', upward)]
    ppermute x0 -> x3, starting transfers between devices: none -> 4.93 us  [the longest x2 3.01 us: per_device(): from_left = lax.ppermute(from_left, 'mode', upward)]
    all_to_all x1, starting transfers between devices: 5.52 us -> 7.46 us  [per_device(): lax.all_to_all(partial_value[None].astype(jnp.bfloat16), 'band', split_ax...]
  transfers between devices with their start and end apart: 4 -> 6, of which waited for: 4 -> 5; matrix products, arithmetic and copies ran while one was open for 0% -> 1% of each run, Pallas kernels for 0% -> 0%
where the time goes in v1:
time: 152 us
  waiting for transfers between devices  84.3 us (55%)
  blocking collectives  17.4 us (11%)
  between operations  14.2 us (9%)
  starting transfers between devices  12.6 us (8%)
  other arithmetic  10.1 us (7%)
  matrix products  10 us (7%)
  local copies, waits for them, and re-layouts  3.13 us (2%)
    all_gather x1, waiting for transfers between devices, per_device(): collected = lax.all_gather(collected, 'band', axis=3, tiled=True)  37.2 us
    reduce_scatter x1, waiting for transfers between devices, per_device(): lax.psum_scatter(partial_terms.astype(jnp.bfloat16), 'mode', scatter_dime...  18.3 us
    ppermute x2, waiting for transfers between devices, per_device(): from_left = lax.ppermute(from_left, 'mode', upward)  14.9 us
    all_to_all x1, waiting for transfers between devices, per_device(): lax.all_to_all(partial_value[None].astype(jnp.bfloat16), 'band', split_ax...  13.8 us
    all_to_all x1, blocking collectives, per_device(): lax.all_to_all(radiation_modes, 'mode', split_axis=0, concat_axis=1, tile...  11.2 us
    cos x1, other arithmetic, make_table(): table = jnp.stack([jnp.cos(angles), -jnp.sin(angles)], axis=1) * norming  9.14 us
    all_to_all x1, starting transfers between devices, per_device(): lax.all_to_all(partial_value[None].astype(jnp.bfloat16), 'band', split_ax...  7.46 us
    all_gather x1, blocking collectives, per_device(): collected = lax.all_gather(forcing, 'mode', axis=1, tiled=True)  6.23 us
  transfers between devices with their start and end apart: 6, of which 5 were waited for; matrix products, arithmetic and copies ran while one was open for 1% of the time, Pallas kernels for 0%

profile of v1, /device:TPU:0, one launch (start us, length us, event | category | flops | bytes accessed | tf_op | source)
XLA Modules:
  0.0 151.8 jit_solution(3906408760266521209)
XLA Ops:
  6.5 9.1 %fusion.21 = (f32[1024,1,512]{0,2,1:T(8,128)S(1)}, f32[1024,1,512]{0,2,1:T(8,128)S(1)}) fusion(s32[512]{0:T(512)} %param.9), kind=kLoop, calls=%fused_computation.29 | loop fusion | flops 7864320 | bytes 4196352 | tf_op jit(solution)/shard_map/cos | solution.py:13
  15.7 0.0 copy-start.1
  15.7 0.8 convolution_convert_fusion
  16.5 0.5 copy-done.2
  17.0 0.6 copy-done.3
  17.6 0.5 collective-permute-start.1
  18.1 1.9 %collective-permute-start = (bf16[1,256,2,512]{1,3,2,0:T(8,128)(2,1)S(1)}, bf16[1,256,2,512]{1,3,2,0:T(8,128)(2,1)S(1)}, u32[]{:S(2)}, u32[]{:S(2)}) collective-permute-start(bf16[1,256,2,512]{1,3,2,0:T(8,128)(2,1)S(1)} %bitcast.81), channel_id=1, source_target_pairs={{0,3},{1,0},{2,1},{3,2},{4,7},{5,4},{6,5},{7,6},{8,11},{9,8},{10,9... | collective-permute-start | bytes 1572872 | tf_op jit(solution)/shard_map/ppermute | solution.py:42
  20.1 0.3 fusion.27
  20.4 9.5 %collective-permute-done.1 = bf16[1,256,2,512]{1,3,2,0:T(8,128)(2,1)S(1)} collective-permute-done((bf16[1,256,2,512]{1,3,2,0:T(8,128)(2,1)S(1)}, bf16[1,256,2,512]{1,3,2,0:T(8,128)(2,1)S(1)}, u32[]{:S(2)}, u32[]{:S(2)}) %collective-permute-start.1) | collective-permute-done | bytes 524320 | tf_op jit(solution)/shard_map/ppermute | solution.py:40
  29.9 2.5 %collective-permute-start.2 = (bf16[1,256,2,512]{1,3,2,0:T(8,128)(2,1)S(1)}, bf16[1,256,2,512]{1,3,2,0:T(8,128)(2,1)S(1)}, u32[]{:S(2)}, u32[]{:S(2)}) collective-permute-start(bf16[1,256,2,512]{1,3,2,0:T(8,128)(2,1)S(1)} %collective-permute-done.1), channel_id=1, source_target_pairs={{0,1},{1,2},{2,3},{3,0},{4,5},{5,6},{6,7},{7,4},{8,9},{9,10},{10,1... | collective-permute-start | bytes 1572872 | tf_op jit(solution)/shard_map/ppermute | solution.py:40
  32.5 0.4 convolution_add_fusion.2
  32.8 0.4 convolution_add_fusion.1
  33.2 5.4 %collective-permute-done.2 = bf16[1,256,2,512]{1,3,2,0:T(8,128)(2,1)S(1)} collective-permute-done((bf16[1,256,2,512]{1,3,2,0:T(8,128)(2,1)S(1)}, bf16[1,256,2,512]{1,3,2,0:T(8,128)(2,1)S(1)}, u32[]{:S(2)}, u32[]{:S(2)}) %collective-permute-start.2) | collective-permute-done | bytes 524320 | tf_op jit(solution)/shard_map/ppermute | solution.py:40
  38.5 0.3 fusion.14
  38.9 1.1 copy.37
  40.0 7.5 %all-to-all-start = ((bf16[1,1,256,2,512]{2,3,1,0,4:T(2,128)(2,1)}), bf16[1,1,256,2,512]{2,3,1,0,4:T(2,128)(2,1)S(1)}, u32[]{:S(2)}, u32[]{:S(2)}) async-start(bf16[1,1,256,2,512]{2,3,1,0,4:T(2,128)(2,1)} %copy.37), calls=%async_computation | async-start | bytes 1048576 | tf_op jit(solution)/shard_map/all_to_all | solution.py:61
  47.5 0.2 reduce-scatter.2.cloned.1.call-start
  48.3 13.8 %all-to-all-done = bf16[1,1,256,2,512]{2,3,1,0,4:T(2,128)(2,1)S(1)} async-done(((bf16[1,1,256,2,512]{2,3,1,0,4:T(2,128)(2,1)}), bf16[1,1,256,2,512]{2,3,1,0,4:T(2,128)(2,1)S(1)}, u32[]{:S(2)}, u32[]{:S(2)}) %all-to-all-start) | async-done | bytes 524320 | tf_op jit(solution)/shard_map/all_to_all | solution.py:61
  62.2 0.1 copy.38
  62.3 0.1 convert_reduce_fusion
  62.4 1.9 %fusion.19 = bf16[1,1024,2,64]{1,3,2,0:T(8,128)(2,1)} fusion(f32[1,1024,256]{2,1,0:T(8,128)S(1)} %copy-done, f32[256,2,64]{0,2,1:T(8,128)S(1)} %convert_reduce_fusion, f32[256]{0:T(256)S(1)} %fusion.43), kind=kOutput, calls=%fused_computation.26 | convolution fusion | flops 402817024 | bytes 1442816 | tf_op jit(solution)/shard_map/ij,wjcf->wicf/dot_general | solution.py:75
  64.3 0.0 reduce-scatter.2.cloned.1.call-update
  64.3 0.0 all-gather.2.cloned.1.call-start
  64.4 18.3 %reduce-scatter.2.cloned.1.call-done = bf16[1,256,2,64]{1,3,2,0:T(8,128)(2,1)} async-done(((bf16[1,1024,2,64]{1,3,2,0:T(8,128)(2,1)}), bf16[1,256,2,64]{1,3,2,0:T(8,128)(2,1)}) %reduce-scatter.2.cloned.1.call-update) | async-done | bytes 65552 | tf_op jit(solution)/shard_map/reduce_scatter | solution.py:78
  82.6 0.9 multiply_convert_fusion
  83.5 6.2 %all_gather.6 = bf16[1,1024,2,64]{1,3,2,0:T(8,128)(2,1)} all-gather(bf16[1,256,2,64]{1,3,2,0:T(8,128)(2,1)S(1)} %multiply_convert_fusion), channel_id=1, replica_groups=mesh['band'=8,'mode'=4] {'mode'}, dimensions={1}, use_global_device_ids=true | all-gather | bytes 327680 | tf_op jit(solution)/shard_map/all_gather | solution.py:82
  89.7 0.0 all-gather.2.cloned.1.call-update
  89.7 11.2 %all_to_all.28 = bf16[4,256,256]{2,1,0:T(8,128)(2,1)S(1)} all-to-all(bf16[4,256,256]{2,1,0:T(8,128)(2,1)S(1)} %bitcast.77), channel_id=1, replica_groups=mesh['band'=8,'mode'=4] {'mode'}, dimensions={0} | all-to-all | bytes 1048576 | tf_op jit(solution)/shard_map/all_to_all | solution.py:84
  101.0 0.4 copy.39
  101.4 0.4 reshape.186
  101.7 37.2 %all-gather.2.cloned.1.call-done = bf16[1,1024,2,512]{1,3,2,0:T(8,128)(2,1)} async-done(((bf16[1,1024,2,64]{1,3,2,0:T(8,128)(2,1)}), bf16[1,1024,2,512]{1,3,2,0:T(8,128)(2,1)}) %all-gather.2.cloned.1.call-update) | async-done | bytes 2097168 | tf_op jit(solution)/shard_map/all_gather | solution.py:83
  139.0 5.9 %fusion.18 = bf16[1,256,1024]{2,1,0:T(8,128)(2,1)} fusion(bf16[256,1024,1]{1,0,2:T(8,128)(2,1)S(1)} %reshape.186, bf16[1,1024,2,512]{1,3,2,0:T(8,128)(2,1)} %all-gather.2.cloned.1.call-done, f32[1024,1,512]{0,2,1:T(8,128)} %copy-done.3, f32[1024,1,512]{0,2,1:T(8,128)} %copy-done.2), kind=kOutput, calls=%fused_computation.24 | convolution fusion | flops 1077411840 | bytes 7340032 | tf_op jit(solution)/shard_map/wpcf,tcf->wpt/dot_general | solution.py:88
  (10 shorter events, 0.0 us)
Async XLA Ops:
  6.5 55.8 %copy-start = (f32[1,1024,256]{2,1,0:T(8,128)S(1)}, f32[1,1024,256]{2,1,0:T(8,128)}, u32[]{:S(2)}) copy-start(f32[1,1024,256]{2,1,0:T(8,128)} %param.7) | copy-start | bytes 3145732
  6.5 9.2 %copy-start.4 = (bf16[1,256,1024]{2,1,0:T(8,128)(2,1)S(1)}, bf16[1,256,1024]{2,1,0:T(8,128)(2,1)}, u32[]{:S(2)}) copy-start(bf16[1,256,1024]{2,1,0:T(8,128)(2,1)} %param.5) | copy-start | bytes 1572868
  15.7 1.3 copy-start.2
  15.7 1.9 %copy-start.3 = (f32[1024,1,512]{0,2,1:T(8,128)}, f32[1024,1,512]{0,2,1:T(8,128)S(1)}, u32[]{:S(2)}) copy-start(f32[1024,1,512]{0,2,1:T(8,128)S(1)} %get-tuple-element.6) | copy-start | bytes 6291460
  15.7 4.3 %copy-start.1 = (bf16[1024,256]{1,0:T(8,128)(2,1)S(1)}, bf16[1024,256]{1,0:T(8,128)(2,1)}, u32[]{:S(2)}) copy-start(bf16[1024,256]{1,0:T(8,128)(2,1)} %param.6) | copy-start | bytes 1572868
  17.6 12.3 %collective-permute-start.1 = (bf16[1,256,2,512]{1,3,2,0:T(8,128)(2,1)S(1)}, bf16[1,256,2,512]{1,3,2,0:T(8,128)(2,1)S(1)}, u32[]{:S(2)}, u32[]{:S(2)}) collective-permute-start(bf16[1,256,2,512]{1,3,2,0:T(8,128)(2,1)S(1)} %bitcast.80), channel_id=1, source_target_pairs={{0,1},{1,2},{2,3},{3,0},{4,5},{5,6},{6,7},{7,4},{8,9},{9,10},{10,1... | collective-permute-start | bytes 1572872 | tf_op jit(solution)/shard_map/ppermute | solution.py:40
  18.1 14.3 %collective-permute-start = (bf16[1,256,2,512]{1,3,2,0:T(8,128)(2,1)S(1)}, bf16[1,256,2,512]{1,3,2,0:T(8,128)(2,1)S(1)}, u32[]{:S(2)}, u32[]{:S(2)}) collective-permute-start(bf16[1,256,2,512]{1,3,2,0:T(8,128)(2,1)S(1)} %bitcast.81), channel_id=1, source_target_pairs={{0,3},{1,0},{2,1},{3,2},{4,7},{5,4},{6,5},{7,6},{8,11},{9,8},{10,9... | collective-permute-start | bytes 1572872 | tf_op jit(solution)/shard_map/ppermute | solution.py:42
  29.9 8.6 %collective-permute-start.2 = (bf16[1,256,2,512]{1,3,2,0:T(8,128)(2,1)S(1)}, bf16[1,256,2,512]{1,3,2,0:T(8,128)(2,1)S(1)}, u32[]{:S(2)}, u32[]{:S(2)}) collective-permute-start(bf16[1,256,2,512]{1,3,2,0:T(8,128)(2,1)S(1)} %collective-permute-done.1), channel_id=1, source_target_pairs={{0,1},{1,2},{2,3},{3,0},{4,5},{5,6},{6,7},{7,4},{8,9},{9,10},{10,1... | collective-permute-start | bytes 1572872 | tf_op jit(solution)/shard_map/ppermute | solution.py:40
  40.0 22.2 %all-to-all-start = ((bf16[1,1,256,2,512]{2,3,1,0,4:T(2,128)(2,1)}), bf16[1,1,256,2,512]{2,3,1,0,4:T(2,128)(2,1)S(1)}, u32[]{:S(2)}, u32[]{:S(2)}) async-start(bf16[1,1,256,2,512]{2,3,1,0,4:T(2,128)(2,1)} %copy.37), calls=%async_computation | async-start | bytes 1048576 | tf_op jit(solution)/shard_map/all_to_all | solution.py:61
  47.5 35.2 %reduce-scatter.2.cloned.1.call-start = ((), (), s32[]{:S(2)}) async-start(), calls=%async_computation.3 | async-start | bytes 327680 | tf_op jit(solution)/shard_map/reduce_scatter | solution.py:78
  64.3 74.7 %all-gather.2.cloned.1.call-start = ((), (), s32[]{:S(2)}) async-start(), calls=%async_computation.4 | async-start | bytes 2359296 | tf_op jit(solution)/shard_map/all_gather | solution.py:83
Sparse Core Ops, SparseCore 0:
  64.4 18.1 reduce-scatter.1
  89.9 49.0 all-gather.1
